TPU v7x, 32 devices: a whole 2x2x4 slice. The times are simulated.
32 devices in a mesh: dp: 8 (over z, x), seq: 4 (over y, core).
Axes of the slice: x: 2, y: 2, z: 4, core: 2. Of those that a mesh axis runs over, the one named last changes fastest.
Arguments:
- inputs: bfloat16 [32, 1024, 1024], P('dp', 'seq'), may hold values from -6 to 6
- norm_gain: float32 [1024], replicated, may hold values from 0.1 to 1.9
- norm_shift: float32 [1024], replicated, may hold values from -3 to 3
- qkv_weight: bfloat16 [1024, 3072], replicated, may hold values from -0.1875 to 0.1875
- out_weight: bfloat16 [1024, 1024], replicated, may hold values from -0.75 to 0.75
- up_weight: bfloat16 [1024, 4096], replicated, may hold values from -0.1875 to 0.1875
- up_bias: float32 [4096], replicated, may hold values from -3 to 3
- down_weight: bfloat16 [4096, 1024], replicated, may hold values from -0.09375 to 0.09375
- down_bias: float32 [1024], replicated, may hold values from -3 to 3
- partners: int32 [32], P('dp'), may hold values from 0 to 31, as said below
- families: int32 [32, 1024], P('dp'), may hold values from 0 to 1023, as said below
- cotangent: bfloat16 [32, 1024, 1024], P('dp', 'seq'), may hold values from -6 to 6
Outputs:
- layer_out: bfloat16 [32, 1024, 1024], P('dp', 'seq')
- input_grad: float32 [32, 1024, 1024], P('dp', 'seq')
- gain_grad: float32 [1024], replicated
- shift_grad: float32 [1024], replicated
- qkv_grad: float32 [1024, 3072], P('dp', 'seq')
- out_grad: float32 [1024, 1024], P('dp', 'seq')
- up_grad: float32 [1024, 4096], P('dp', 'seq')
- up_bias_grad: float32 [4096], replicated
- down_grad: float32 [4096, 1024], P('dp', 'seq')
- down_bias_grad: float32 [1024], replicated
Inputs may be any that keep to these rules, and one draw needn't show every extreme that they name: partners pairs the rows of each aligned block of 4 rows two by two: partners[partners[r]] = r, partners[r] != r, and partners[r] lies in the block of r. `families`: family ids never fall along a row and the last position of every row has id 1024 - 1; in each aligned block of 4 rows at least one row is a single group over all 1024 positions.
All inputs are finite; a program needn't handle non-finite values.
Results may differ from a plain program's by a relative error of at most 0.0099.
Values may be sent and summed in bfloat16 or wider, within the bound.
A program may use at most 256 MiB of HBM per device.

v0:
```python
import jax
import jax.numpy as jnp
from jax import lax
from jax.sharding import PartitionSpec as P

HEADS = 16
HEAD_DIM = 64
ROT = 32
EPS = 1e-05


def norm_piece(values, norm_gain, norm_shift):
    row_mean = jnp.mean(values, -1, keepdims=True)
    centered = values - row_mean
    variance = jnp.mean(centered * centered, -1, keepdims=True)
    return centered * lax.rsqrt(variance + EPS) * norm_gain + norm_shift


def rotate(values, places):
    half_rot = ROT // 2
    inverse_freq = 10000.0 ** (-2.0 * jnp.arange(half_rot).astype(jnp.float32) / ROT)
    angles = places.astype(jnp.float32)[:, None] * inverse_freq[None, :]
    cosine_table = jnp.cos(angles)[:, None, :]
    sine_table = jnp.sin(angles)[:, None, :]
    first_half = values[..., :half_rot]
    second_half = values[..., half_rot:ROT]
    return jnp.concatenate(
        [
            first_half * cosine_table - second_half * sine_table,
            second_half * cosine_table + first_half * sine_table,
            values[..., ROT:],
        ],
        -1,
    )


def gelu_piece(values):
    return jax.nn.gelu(values, approximate=True)


def masked_scores(queries, key_rows, family):
    scaling = HEAD_DIM ** (-0.5)
    scores = (
        jnp.einsum("qhd,khd->hqk", queries, key_rows, preferred_element_type=jnp.float32) * scaling
    )
    places = jnp.arange(queries.shape[0])
    allowed = (places[None, :] <= places[:, None]) & (family[:, None] == family[None, :])
    return jnp.where(allowed[None], scores, -1000000000.0)


def forward_row(pieces):
    qkv_rows, family = pieces
    scores = masked_scores(qkv_rows[:, 0], qkv_rows[:, 1], family)
    row_max = jnp.max(scores, -1, keepdims=True)
    weights = jnp.exp(scores - row_max)
    row_total = jnp.sum(weights, -1, keepdims=True)
    prob_low = (weights / row_total).astype(jnp.bfloat16)
    mixed_heads = jnp.einsum(
        "hqk,khd->qhd", prob_low, qkv_rows[:, 2], preferred_element_type=jnp.float32
    )
    return (mixed_heads.astype(jnp.bfloat16), (row_max + jnp.log(row_total))[..., 0])


def backward_row(pieces):
    qkv_rows, family, log_total, d_mixed = pieces
    scaling = HEAD_DIM ** (-0.5)
    queries = qkv_rows[:, 0]
    key_rows = qkv_rows[:, 1]
    value_rows = qkv_rows[:, 2]
    scores = masked_scores(queries, key_rows, family)
    chances = jnp.exp(scores - log_total[..., None])
    d_chances = jnp.einsum("qhd,khd->hqk", d_mixed, value_rows, preferred_element_type=jnp.float32)
    d_scores = (chances * (d_chances - jnp.sum(chances * d_chances, -1, keepdims=True))).astype(
        jnp.bfloat16
    )
    d_value = jnp.einsum(
        "hqk,qhd->khd", chances.astype(jnp.bfloat16), d_mixed, preferred_element_type=jnp.float32
    )
    d_query = (
        jnp.einsum("hqk,khd->qhd", d_scores, key_rows, preferred_element_type=jnp.float32) * scaling
    )
    d_key = (
        jnp.einsum("hqk,qhd->khd", d_scores, queries, preferred_element_type=jnp.float32) * scaling
    )
    return jnp.stack([d_query, d_key, d_value], 1).astype(jnp.bfloat16)


def on_device(
    inputs,
    norm_gain,
    norm_shift,
    qkv_weight,
    out_weight,
    up_weight,
    up_bias,
    down_weight,
    down_bias,
    partners,
    families,
    cotangent,
):
    row_count, place_count, model_width = inputs.shape
    seq_size = lax.axis_size("seq")
    token_count = row_count * place_count
    values = inputs.astype(jnp.float32)
    normed, norm_pull = jax.vjp(norm_piece, values, norm_gain, norm_shift)
    normed_low = normed.astype(jnp.bfloat16).reshape(token_count, model_width)
    raw_qkv = jnp.dot(normed_low, qkv_weight, preferred_element_type=jnp.float32)
    raw_qkv = raw_qkv.reshape(row_count, place_count, 3, HEADS, HEAD_DIM)
    places = lax.axis_index("seq") * place_count + jnp.arange(place_count)

    def rope_piece(raw_values):
        return jnp.stack(
            [
                rotate(raw_values[:, :, 0], places),
                rotate(raw_values[:, :, 1], places),
                raw_values[:, :, 2],
            ],
            2,
        )

    rotated, rope_pull = jax.vjp(rope_piece, raw_qkv)
    outgoing = rotated.astype(jnp.bfloat16).reshape(row_count, place_count, 3, seq_size, -1)
    received = lax.all_to_all(outgoing, "seq", split_axis=3, concat_axis=1, tiled=True)
    full_length = received.shape[1]
    received = received.reshape(row_count, full_length, 3, -1, HEAD_DIM)
    mixed_heads, log_totals = lax.map(forward_row, (received, families))
    group_width = mixed_heads.shape[2] * HEAD_DIM
    returned = lax.all_to_all(
        mixed_heads.reshape(row_count, full_length, 1, group_width),
        "seq",
        split_axis=1,
        concat_axis=2,
        tiled=True,
    )
    heads_low = returned.reshape(token_count, model_width)
    attn_out = jnp.dot(heads_low, out_weight, preferred_element_type=jnp.float32)
    hidden = jnp.dot(normed_low, up_weight, preferred_element_type=jnp.float32) + up_bias
    active, gelu_pull = jax.vjp(gelu_piece, hidden)
    active_low = active.astype(jnp.bfloat16)
    mlp_out = jnp.dot(active_low, down_weight, preferred_element_type=jnp.float32) + down_bias
    layer_out = (
        (values.reshape(token_count, model_width) + attn_out + mlp_out)
        .astype(jnp.bfloat16)
        .reshape(inputs.shape)
    )
    local_rows = partners - lax.axis_index("dp") * row_count
    grad_low = jnp.take(cotangent, local_rows, axis=0).reshape(token_count, model_width)
    down_grad = jnp.einsum("tf,td->fd", active_low, grad_low, preferred_element_type=jnp.float32)
    down_bias_grad = jnp.sum(grad_low.astype(jnp.float32), 0)
    out_grad = jnp.einsum("te,td->ed", heads_low, grad_low, preferred_element_type=jnp.float32)
    d_active = jnp.einsum("td,fd->tf", grad_low, down_weight, preferred_element_type=jnp.float32)
    d_hidden_low = gelu_pull(d_active)[0].astype(jnp.bfloat16)
    up_bias_grad = jnp.sum(d_hidden_low.astype(jnp.float32), 0)
    up_grad = jnp.einsum("td,tf->df", normed_low, d_hidden_low, preferred_element_type=jnp.float32)
    d_heads = jnp.einsum(
        "td,ed->te", grad_low, out_weight, preferred_element_type=jnp.float32
    ).astype(jnp.bfloat16)
    d_heads = d_heads.reshape(row_count, place_count, seq_size, group_width)
    d_heads_split = lax.all_to_all(d_heads, "seq", split_axis=2, concat_axis=1, tiled=True)
    d_heads_split = d_heads_split.reshape(row_count, full_length, -1, HEAD_DIM)
    d_blocks = lax.map(backward_row, (received, families, log_totals, d_heads_split))
    d_blocks = d_blocks.reshape(row_count, full_length, 3, 1, group_width)
    d_rotated = lax.all_to_all(d_blocks, "seq", split_axis=1, concat_axis=3, tiled=True)
    d_rotated = d_rotated.reshape(row_count, place_count, 3, HEADS, HEAD_DIM).astype(jnp.float32)
    d_raw_low = rope_pull(d_rotated)[0].astype(jnp.bfloat16).reshape(token_count, 3 * model_width)
    qkv_grad = jnp.einsum("td,te->de", normed_low, d_raw_low, preferred_element_type=jnp.float32)
    d_normed = jnp.einsum("te,de->td", d_raw_low, qkv_weight, preferred_element_type=jnp.float32)
    d_normed = d_normed + jnp.einsum(
        "tf,df->td", d_hidden_low, up_weight, preferred_element_type=jnp.float32
    )
    d_values, gain_grad, shift_grad = norm_pull(d_normed.reshape(inputs.shape))
    input_grad = grad_low.astype(jnp.float32).reshape(inputs.shape) + d_values
    gain_sum, shift_sum, up_bias_sum, down_bias_sum = lax.psum(
        (gain_grad, shift_grad, up_bias_grad, down_bias_grad), ("dp", "seq")
    )
    partial_sums = (
        lax.psum_scatter(qkv_grad, "seq", scatter_dimension=1, tiled=True),
        lax.psum_scatter(out_grad, "seq", scatter_dimension=1, tiled=True),
        lax.psum_scatter(up_grad, "seq", scatter_dimension=1, tiled=True),
        lax.psum_scatter(down_grad, "seq", scatter_dimension=1, tiled=True),
    )
    qkv_sum, out_sum, up_sum, down_sum = (
        lax.psum_scatter(partial_sums[0], "dp", scatter_dimension=0, tiled=True),
        lax.psum_scatter(partial_sums[1], "dp", scatter_dimension=0, tiled=True),
        lax.psum_scatter(partial_sums[2], "dp", scatter_dimension=0, tiled=True),
        lax.psum_scatter(partial_sums[3], "dp", scatter_dimension=0, tiled=True),
    )
    return (
        layer_out,
        input_grad,
        gain_sum,
        shift_sum,
        qkv_sum,
        out_sum,
        up_sum,
        up_bias_sum,
        down_sum,
        down_bias_sum,
    )


def solution(mesh):
    placed = (
        P("dp", "seq", None),
        P(),
        P(),
        P(),
        P(),
        P(),
        P(),
        P(),
        P(),
        P("dp"),
        P("dp", None),
        P("dp", "seq", None),
    )
    return jax.shard_map(
        on_device,
        mesh=mesh,
        in_specs=placed,
        out_specs=(
            P("dp", "seq", None),
            P("dp", "seq", None),
            P(),
            P(),
            P("dp", "seq"),
            P("dp", "seq"),
            P("dp", "seq"),
            P(),
            P("dp", "seq"),
            P(),
        ),
        check_vma=False,
    )
```

profile of v0, /device:TPU:0, one launch (start us, length us, event | category | flops | bytes accessed | tf_op | source)
XLA Modules:
  0.0 1331.5 jit_solution(15439892296866444212)
XLA Ops:
  48.4 10.8 fusion.39
  96.9 58.3 %all-to-all-done = bf16[4,256,3,4,256]{1,4,0,2,3:T(8,128)(2,1)} async-done(((bf16[4,256,3,4,256]{1,4,0,2,3:T(8,128)(2,1)}), bf16[4,256,3,4,256]{1,4,0,2,3:T(8,128)(2,1)}, u32[]{:S(2)}, u32[]{:S(2)}) %all-to-all-start) | async-done | bytes 6291488 | tf_op jit(solution)/shard_map/all_to_all | solution.py:124
  155.2 10.3 copy.112
  165.4 11.0 reshape.385
  176.4 60.7 %while.22 = (s32[]{:T(128)}, bf16[4,1024,4,64]{1,3,2,0:T(8,128)(2,1)}, f32[4,4,1024]{2,1,0:T(4,128)}, bf16[4,1024,3,4,64]{1,4,3,2,0:T(8,128)(2,1)}, s32[4,1024]{1,0:T(4,128)S(1)}, /*index=5*/s32[]{:T(128)}) while((s32[]{:T(128)}, bf16[4,1024,4,64]{1,3,2,0:T(8,128)(2,1)}, f32[4,4,1024]{2,1,0:T(4,128)}, bf16[4,1024,3,4,64]{1,4,3,2,0:T(8,128)(2,1)}, ...), condition=%wide.region_5.6_spmd, body=%wide.region_2.5_spmd.sunk | while | flops 1127477248 | bytes 59913292 | solution.py:127
  246.0 208.5 %while.23 = (s32[]{:T(128)}, bf16[4,1024,3,4,64]{1,4,3,2,0:T(8,128)(2,1)}, bf16[4,1024,3,4,64]{1,4,3,2,0:T(8,128)(2,1)}, s32[4,1024]{1,0:T(4,128)S(1)}, f32[4,4,...) while((s32[]{:T(128)}, bf16[4,1024,3,4,64]{1,4,3,2,0:T(8,128)(2,1)}, ...), condition=%wide.region_8.9_spmd, body=%wide.region_6.8_spmd.sunk | while | flops 2731274240 | bytes 196179696 | solution.py:162
  258.5 12.7 multiply_reduce_fusion.5
  271.2 11.9 multiply_convert_fusion.5
  310.6 12.7 multiply_reduce_fusion.5
  323.3 11.9 multiply_convert_fusion.5
  362.7 12.7 multiply_reduce_fusion.5
  375.4 11.9 multiply_convert_fusion.5
  414.8 12.7 multiply_reduce_fusion.5
  427.5 11.9 multiply_convert_fusion.5
  454.5 10.8 copy.118
  480.8 82.8 %all-to-all-done.3 = bf16[4,1024,3,1,256]{4,0,3,2,1:T(4,128)(2,1)} async-done(((bf16[4,1024,3,1,256]{4,0,3,2,1:T(4,128)(2,1)}), bf16[4,1024,3,1,256]{4,0,3,2,1:T(4,128)(2,1)}, u32[]{:S(2)}, u32[]{:S(2)}) %all-to-all-start.3) | async-done | bytes 6291488 | tf_op jit(solution)/shard_map/all_to_all | solution.py:164
  573.6 12.6 copy.120
  609.6 11.5 copy.121
  638.2 18.6 %fusion.48 = f32[1024,4096]{1,0:T(8,128)} fusion(bf16[1024,1024]{1,0:T(8,128)(2,1)} %bitcast.215, bf16[1024,4096]{1,0:T(8,128)(2,1)} %param.21), kind=kOutput, calls=%fused_computation.117 | convolution fusion | flops 8589934592 | bytes 27262976 | tf_op jit(solution)/shard_map/dot_general | solution.py:138
  656.8 26.5 %convert_reduce_fusion = (f32[4096]{0:T(1024)S(1)}, bf16[1024,4096]{1,0:T(8,128)(2,1)}) fusion(f32[1024,4096]{1,0:T(8,128)} %fusion.48, f32[4096]{0:T(1024)S(1)} %copy-done.28, bf16[1024,1024]{1,0:T(8,128)(2,1)} %copy-done.9, bf16[4096,1024]{1,0:T(8,128)(2,1)} %param.23), kind=kOutput, calls=%fused_computation.59 | convolution fusion | flops 8686399488 | bytes 35684352 | tf_op jit(solution)/shard_map/td,fd->tf/dot_general | solution.py:152
  683.3 16.3 %fusion.52 = f32[1024,4096]{1,0:T(8,128)} fusion(bf16[1024,1024]{1,0:T(8,128)(2,1)} %bitcast.216, bf16[1024,4096]{1,0:T(8,128)(2,1)} %get-tuple-element.104), kind=kOutput, calls=%fused_computation.121 | convolution fusion | flops 8589934592 | bytes 27262976 | tf_op jit(solution)/shard_map/td,tf->df/dot_general | solution.py:155
  699.7 20.1 %fusion.43 = f32[4096,1024]{1,0:T(8,128)} fusion(bf16[1024,1024]{1,0:T(8,128)(2,1)} %copy-done.9, f32[1024,4096]{1,0:T(8,128)} %fusion.48, f32[4096]{0:T(1024)S(1)} %copy-done.28), kind=kOutput, calls=%fused_computation.113 | convolution fusion | flops 8631877632 | bytes 35667968 | tf_op jit(solution)/shard_map/tf,td->fd/dot_general | solution.py:149
  720.5 17.9 %reduce-scatter.9.cloned.1.call-done = f32[1024,768]{1,0:T(8,128)} async-done(((f32[1024,3072]{1,0:T(8,128)}), f32[1024,768]{1,0:T(8,128)}) %reduce-scatter.9.cloned.1.call-update) | async-done | bytes 3145744 | tf_op jit(solution)/shard_map/reduce_scatter | solution.py:178
  738.5 128.8 %reduce-scatter.17.cloned.1.call-done = f32[1024,1024]{1,0:T(8,128)} async-done(((f32[1024,4096]{1,0:T(8,128)}), f32[1024,1024]{1,0:T(8,128)}) %reduce-scatter.17.cloned.1.call-update) | async-done | bytes 4194320 | tf_op jit(solution)/shard_map/reduce_scatter | solution.py:180
  873.3 122.5 %reduce-scatter.21.cloned.1.call-done = f32[4096,256]{1,0:T(8,128)} async-done(((f32[4096,1024]{1,0:T(8,128)}), f32[4096,256]{1,0:T(8,128)}) %reduce-scatter.21.cloned.1.call-update) | async-done | bytes 4194320 | tf_op jit(solution)/shard_map/reduce_scatter | solution.py:181
  995.9 19.7 %fusion.38 = bf16[1024,1024]{1,0:T(8,128)(2,1)} fusion(f32[1024,1024]{1,0:T(8,128)} %fusion.47, bf16[4,256,1024]{2,1,0:T(8,128)(2,1)} %param.16, f32[1024]{0:T(1024)S(1)} %copy-done.29, bf16[4096,1024]{1,0:T(8,128)(2,1)} %param.23, f32[1024,4096]{1,0:T(8,128)} %fusion.48, f32[4096]{0:T(1024)S(1)} %copy-done.28), kind=kOutput, calls=%fused_computation.74 | convolution fusion | flops 8637120512 | bytes 33574912 | tf_op jit(solution)/shard_map/dot_general | solution.py:141
  1015.5 10.7 fusion.49
  1026.3 14.2 %fusion.46 = (f32[1024]{0:T(1024)S(1)}, f32[1024,1024]{1,0:T(8,128)S(1)}) fusion(f32[1024,1024]{1,0:T(8,128)S(1)} %fusion.49, bf16[1024,4096]{1,0:T(8,128)(2,1)} %get-tuple-element.104, bf16[1024,4096]{1,0:T(8,128)(2,1)} %param.21), kind=kOutput, calls=%fused_computation.115 | convolution fusion | flops 8592030720 | bytes 25169920 | tf_op jit(solution)/shard_map/tf,df->td/dot_general | solution.py:169
  1043.5 40.4 %all-reduce.9 = (f32[1024]{0:T(1024)}, f32[1024]{0:T(1024)}, f32[4096]{0:T(1024)}, f32[1024]{0:T(1024)}) all-reduce(f32[1024]{0:T(1024)S(1)} %get-tuple-element.73, f32[1024]{0:T(1024)S(1)} %get-tuple-element.130, f32[4096]{0:T(1024)S(1)} %get-tuple-element.103, f32[1024]{0:T(1024)S(1)} %copy-done.26), channel_id=1, replica_groups=mesh['dp'=8,'seq'=4] {'dp','seq'}, use_global_device_ids=true, to_apply=%region_12.13 | all-reduce | flops 7168 | bytes 57344 | tf_op jit(solution)/shard_map/psum | solution.py:174
  1089.6 51.3 %reduce-scatter.11.cloned.1.call-done = f32[128,768]{1,0:T(8,128)} async-done(((f32[1024,768]{1,0:T(8,128)}), f32[128,768]{1,0:T(8,128)}) %reduce-scatter.11.cloned.1.call-update) | async-done | bytes 393232 | tf_op jit(solution)/shard_map/reduce_scatter | solution.py:184
  1140.9 91.2 %reduce-scatter.19.cloned.1.call-done = f32[128,1024]{1,0:T(8,128)} async-done(((f32[1024,1024]{1,0:T(8,128)}), f32[128,1024]{1,0:T(8,128)}) %reduce-scatter.19.cloned.1.call-update) | async-done | bytes 524304 | tf_op jit(solution)/shard_map/reduce_scatter | solution.py:186
  1232.1 92.3 %reduce-scatter.23.cloned.1.call-done = f32[512,256]{1,0:T(8,128)} async-done(((f32[4096,256]{1,0:T(8,128)}), f32[512,256]{1,0:T(8,128)}) %reduce-scatter.23.cloned.1.call-update) | async-done | bytes 524304 | tf_op jit(solution)/shard_map/reduce_scatter | solution.py:187
  (244 shorter events, 339.2 us)
Async XLA Ops:
  26.4 51.6 %all-to-all-start.2 = ((bf16[4,256,4,256]{3,1,0,2:T(8,128)(2,1)}), bf16[4,256,4,256]{3,1,0,2:T(8,128)(2,1)}, u32[]{:S(2)}, u32[]{:S(2)}) async-start(bf16[4,256,4,256]{3,1,0,2:T(8,128)(2,1)} %copy.116), calls=%async_computation.2 | async-start | bytes 4194304 | tf_op jit(solution)/shard_map/all_to_all | solution.py:160
  33.1 11.6 copy-start.17
  78.0 77.2 %all-to-all-start = ((bf16[4,256,3,4,256]{1,4,0,2,3:T(8,128)(2,1)}), bf16[4,256,3,4,256]{1,4,0,2,3:T(8,128)(2,1)}, u32[]{:S(2)}, u32[]{:S(2)}) async-start(bf16[4,256,3,4,256]{1,4,0,2,3:T(8,128)(2,1)} %copy.127), calls=%async_computation | async-start | bytes 12582912 | tf_op jit(solution)/shard_map/all_to_all | solution.py:124
  165.4 11.0 copy-start.19
  241.4 223.9 %all-to-all-start.1 = ((bf16[4,1024,1,256]{3,0,2,1:T(4,128)(2,1)}), bf16[4,1024,1,256]{3,0,2,1:T(4,128)(2,1)}, u32[]{:S(2)}, u32[]{:S(2)}) async-start(bf16[4,1024,1,256]{3,0,2,1:T(4,128)(2,1)} %copy.113), calls=%async_computation.1 | async-start | bytes 4194304 | tf_op jit(solution)/shard_map/all_to_all | solution.py:129
  271.2 20.0 %slice-start = ((s8[16777216]{0:T(1024)(128)(4,1)}), s8[4194304]{0:T(1024)(128)(4,1)S(1)}, s32[]{:S(2)}) async-start(s8[16777216]{0:T(1024)(128)(4,1)} %bitcast.198), calls=%async_computation.20 | async-start | bytes 8388608 | tf_op jit(solution)/shard_map/while
  271.2 20.0 %slice-start.1 = ((s8[16777216]{0:T(1024)(128)(4,1)}), s8[4194304]{0:T(1024)(128)(4,1)S(1)}, s32[]{:S(2)}) async-start(s8[16777216]{0:T(1024)(128)(4,1)} %bitcast.198), calls=%async_computation.21 | async-start | bytes 8388608 | tf_op jit(solution)/shard_map/while
  271.2 20.0 %slice-start.2 = ((s8[16777216]{0:T(1024)(128)(4,1)}), s8[4194304]{0:T(1024)(128)(4,1)S(1)}, s32[]{:S(2)}) async-start(s8[16777216]{0:T(1024)(128)(4,1)} %bitcast.198), calls=%async_computation.22 | async-start | bytes 8388608 | tf_op jit(solution)/shard_map/while
  299.7 10.9 copy-start.1
  323.2 20.0 %slice-start = ((s8[16777216]{0:T(1024)(128)(4,1)}), s8[4194304]{0:T(1024)(128)(4,1)S(1)}, s32[]{:S(2)}) async-start(s8[16777216]{0:T(1024)(128)(4,1)} %bitcast.198), calls=%async_computation.20 | async-start | bytes 8388608 | tf_op jit(solution)/shard_map/while
  323.3 20.0 %slice-start.1 = ((s8[16777216]{0:T(1024)(128)(4,1)}), s8[4194304]{0:T(1024)(128)(4,1)S(1)}, s32[]{:S(2)}) async-start(s8[16777216]{0:T(1024)(128)(4,1)} %bitcast.198), calls=%async_computation.21 | async-start | bytes 8388608 | tf_op jit(solution)/shard_map/while
  323.3 20.0 %slice-start.2 = ((s8[16777216]{0:T(1024)(128)(4,1)}), s8[4194304]{0:T(1024)(128)(4,1)S(1)}, s32[]{:S(2)}) async-start(s8[16777216]{0:T(1024)(128)(4,1)} %bitcast.198), calls=%async_computation.22 | async-start | bytes 8388608 | tf_op jit(solution)/shard_map/while
  375.4 20.0 %slice-start = ((s8[16777216]{0:T(1024)(128)(4,1)}), s8[4194304]{0:T(1024)(128)(4,1)S(1)}, s32[]{:S(2)}) async-start(s8[16777216]{0:T(1024)(128)(4,1)} %bitcast.198), calls=%async_computation.20 | async-start | bytes 8388608 | tf_op jit(solution)/shard_map/while
  375.4 20.0 %slice-start.1 = ((s8[16777216]{0:T(1024)(128)(4,1)}), s8[4194304]{0:T(1024)(128)(4,1)S(1)}, s32[]{:S(2)}) async-start(s8[16777216]{0:T(1024)(128)(4,1)} %bitcast.198), calls=%async_computation.21 | async-start | bytes 8388608 | tf_op jit(solution)/shard_map/while
  375.4 20.0 %slice-start.2 = ((s8[16777216]{0:T(1024)(128)(4,1)}), s8[4194304]{0:T(1024)(128)(4,1)S(1)}, s32[]{:S(2)}) async-start(s8[16777216]{0:T(1024)(128)(4,1)} %bitcast.198), calls=%async_computation.22 | async-start | bytes 8388608 | tf_op jit(solution)/shard_map/while
  427.5 20.0 %slice-start = ((s8[16777216]{0:T(1024)(128)(4,1)}), s8[4194304]{0:T(1024)(128)(4,1)S(1)}, s32[]{:S(2)}) async-start(s8[16777216]{0:T(1024)(128)(4,1)} %bitcast.198), calls=%async_computation.20 | async-start | bytes 8388608 | tf_op jit(solution)/shard_map/while
  427.5 20.0 %slice-start.1 = ((s8[16777216]{0:T(1024)(128)(4,1)}), s8[4194304]{0:T(1024)(128)(4,1)S(1)}, s32[]{:S(2)}) async-start(s8[16777216]{0:T(1024)(128)(4,1)} %bitcast.198), calls=%async_computation.21 | async-start | bytes 8388608 | tf_op jit(solution)/shard_map/while
  427.5 20.0 %slice-start.2 = ((s8[16777216]{0:T(1024)(128)(4,1)}), s8[4194304]{0:T(1024)(128)(4,1)S(1)}, s32[]{:S(2)}) async-start(s8[16777216]{0:T(1024)(128)(4,1)} %bitcast.198), calls=%async_computation.22 | async-start | bytes 8388608 | tf_op jit(solution)/shard_map/while
  465.2 98.4 %all-to-all-start.3 = ((bf16[4,1024,3,1,256]{4,0,3,2,1:T(4,128)(2,1)}), bf16[4,1024,3,1,256]{4,0,3,2,1:T(4,128)(2,1)}, u32[]{:S(2)}, u32[]{:S(2)}) async-start(bf16[4,1024,3,1,256]{4,0,3,2,1:T(4,128)(2,1)} %copy.118), calls=%async_computation.3 | async-start | bytes 12582912 | tf_op jit(solution)/shard_map/all_to_all | solution.py:164
  470.5 249.4 %reduce-scatter.13.cloned.1.call-start = ((), (), s32[]{:S(2)}) async-start(), calls=%async_computation.14 | async-start | bytes 5242880 | tf_op jit(solution)/shard_map/reduce_scatter | solution.py:179
  480.8 257.6 %reduce-scatter.9.cloned.1.call-start = ((), (), s32[]{:S(2)}) async-start(), calls=%async_computation.12 | async-start | bytes 15728640 | tf_op jit(solution)/shard_map/reduce_scatter | solution.py:178
  638.1 18.7 %copy-start.28 = (f32[4096]{0:T(1024)S(1)}, f32[4096]{0:T(1024)}, u32[]{:S(2)}) copy-start(f32[4096]{0:T(1024)} %param.22) | copy-start | bytes 49156
  638.1 229.2 %reduce-scatter.17.cloned.1.call-start = ((), (), s32[]{:S(2)}) async-start(), calls=%async_computation.16 | async-start | bytes 20971520 | tf_op jit(solution)/shard_map/reduce_scatter | solution.py:180
  699.7 296.2 %reduce-scatter.21.cloned.1.call-start = ((), (), s32[]{:S(2)}) async-start(), calls=%async_computation.18 | async-start | bytes 20971520 | tf_op jit(solution)/shard_map/reduce_scatter | solution.py:181
  719.8 369.7 %reduce-scatter.15.cloned.1.call-start = ((), (), s32[]{:S(2)}) async-start(), calls=%async_computation.15 | async-start | bytes 1179648 | tf_op jit(solution)/shard_map/reduce_scatter | solution.py:185
  720.4 420.5 %reduce-scatter.11.cloned.1.call-start = ((), (), s32[]{:S(2)}) async-start(), calls=%async_computation.13 | async-start | bytes 3538944 | tf_op jit(solution)/shard_map/reduce_scatter | solution.py:184
  738.4 493.7 %reduce-scatter.19.cloned.1.call-start = ((), (), s32[]{:S(2)}) async-start(), calls=%async_computation.17 | async-start | bytes 4718592 | tf_op jit(solution)/shard_map/reduce_scatter | solution.py:186
  867.3 457.1 %reduce-scatter.23.cloned.1.call-start = ((), (), s32[]{:S(2)}) async-start(), calls=%async_computation.19 | async-start | bytes 4718592 | tf_op jit(solution)/shard_map/reduce_scatter | solution.py:187
  873.3 122.6 %copy-start.29 = (f32[1024]{0:T(1024)S(1)}, f32[1024]{0:T(1024)}, u32[]{:S(2)}) copy-start(f32[1024]{0:T(1024)} %param.24) | copy-start | bytes 12292
  1026.3 14.2 %copy-start.2 = (bf16[4,256,1024]{2,1,0:T(8,128)(2,1)S(1)}, bf16[4,256,1024]{2,1,0:T(8,128)(2,1)}, u32[]{:S(2)}) copy-start(bf16[4,256,1024]{2,1,0:T(8,128)(2,1)} %param.16) | copy-start | bytes 6291460
  1026.3 14.2 %copy-start.18 = (f32[4,256]{1,0:T(4,128)S(1)}, f32[4,256]{1,0:T(4,128)}, u32[]{:S(2)}) copy-start(f32[4,256]{1,0:T(4,128)} %copy-done.17) | copy-start | bytes 12292
  1026.3 14.2 %copy-start.23 = (f32[1024]{0:T(1024)S(1)}, f32[1024]{0:T(1024)}, u32[]{:S(2)}) copy-start(f32[1024]{0:T(1024)} %param.17) | copy-start | bytes 12292
  (29 other events, 143.3 us)
Sparse Core Ops, SparseCore 0:
  480.9 69.5 reduce-scatter.12
  638.2 100.1 reduce-scatter.8
  741.1 126.0 reduce-scatter.16
  869.7 126.0 reduce-scatter.20
  1000.0 63.4 reduce-scatter.14
  1067.6 73.3 reduce-scatter.10
  1145.1 86.9 reduce-scatter.18
  1236.7 87.6 reduce-scatter.22
where the time goes:
time: 1340 us; the launch traced here: 1330 us
  waiting for transfers between devices  646 us (48%)
  matrix products  334 us (25%)
  local copies, waits for them, and re-layouts  152 us (11%)
  other arithmetic  123 us (9%)
  blocking collectives  40.4 us (3%)
  starting transfers between devices  21.1 us (2%)
  between operations  14.8 us (1%)
    reduce_scatter x1, waiting for transfers between devices, on_device(): lax.psum_scatter(up_grad, 'seq', scatter_dimension=1, tiled=True)  129 us
    reduce_scatter x1, waiting for transfers between devices, on_device(): lax.psum_scatter(down_grad, 'seq', scatter_dimension=1, tiled=True)  123 us
    reduce_scatter x1, waiting for transfers between devices, on_device(): lax.psum_scatter(partial_sums[3], 'dp', scatter_dimension=0, tiled=True)  92.3 us
    reduce_scatter x1, waiting for transfers between devices, on_device(): lax.psum_scatter(partial_sums[2], 'dp', scatter_dimension=0, tiled=True)  91.2 us
    all_to_all x1, waiting for transfers between devices, on_device(): lax.all_to_all(d_blocks, 'seq', split_axis=1, concat_axis=3, tiled=True)  82.8 us
    dot_general x8, matrix products, masked_scores(): jnp.einsum('qhd,khd->hqk', queries, key_rows, preferred_element_type=jnp....  62.9 us
    all_to_all x1, waiting for transfers between devices, on_device(): lax.all_to_all(outgoing, 'seq', split_axis=3, concat_axis=1, tiled=True)  58.3 us
    reduce_scatter x1, waiting for transfers between devices, on_device(): lax.psum_scatter(partial_sums[0], 'dp', scatter_dimension=0, tiled=True)  51.3 us
  transfers between devices with their start and end apart: 12, of which 8 were waited for; matrix products, arithmetic and copies ran while one was open for 37% of the time, Pallas kernels for 0%

commit v1 on v0

--- a/solution.py
+++ b/solution.py
@@ -172,7 +172,7 @@
     d_values, gain_grad, shift_grad = norm_pull(d_normed.reshape(inputs.shape))
     input_grad = grad_low.astype(jnp.float32).reshape(inputs.shape) + d_values
     gain_sum, shift_sum, up_bias_sum, down_bias_sum = lax.psum(
-        (gain_grad, shift_grad, up_bias_grad, down_bias_grad), ("dp", "seq")
+        lax.psum((gain_grad, shift_grad, up_bias_grad, down_bias_grad), "seq"), "dp"
     )
     partial_sums = (
         lax.psum_scatter(qkv_grad, "seq", scatter_dimension=1, tiled=True),

time: 1340 us -> 1340 us (level)
    psum x1 -> x2, blocking collectives: 40.4 us -> 48.8 us  [the longest x1 38.5 us: on_device(): lax.psum(lax.psum((gain_grad, shift_grad, up_bias_grad, down_bias_grad),...]
where the time goes in v1:
time: 1340 us; the launch traced here: 1330 us
  waiting for transfers between devices  638 us (48%)
  matrix products  334 us (25%)
  local copies, waits for them, and re-layouts  152 us (11%)
  other arithmetic  123 us (9%)
  blocking collectives  48.8 us (4%)
  starting transfers between devices  21.1 us (2%)
  between operations  14.9 us (1%)
    reduce_scatter x1, waiting for transfers between devices, on_device(): lax.psum_scatter(up_grad, 'seq', scatter_dimension=1, tiled=True)  129 us
    reduce_scatter x1, waiting for transfers between devices, on_device(): lax.psum_scatter(down_grad, 'seq', scatter_dimension=1, tiled=True)  123 us
    reduce_scatter x1, waiting for transfers between devices, on_device(): lax.psum_scatter(partial_sums[3], 'dp', scatter_dimension=0, tiled=True)  92.3 us
    reduce_scatter x1, waiting for transfers between devices, on_device(): lax.psum_scatter(partial_sums[2], 'dp', scatter_dimension=0, tiled=True)  91.4 us
    all_to_all x1, waiting for transfers between devices, on_device(): lax.all_to_all(d_blocks, 'seq', split_axis=1, concat_axis=3, tiled=True)  82.8 us
    dot_general x8, matrix products, masked_scores(): jnp.einsum('qhd,khd->hqk', queries, key_rows, preferred_element_type=jnp....  62.9 us
    all_to_all x1, waiting for transfers between devices, on_device(): lax.all_to_all(outgoing, 'seq', split_axis=3, concat_axis=1, tiled=True)  58.3 us
    convert_element_type x4, other arithmetic, backward_row(): (chances * (d_chances - jnp.sum(chances * d_chances, -1, keepdims=True)))...  47.6 us
  transfers between devices with their start and end apart: 12, of which 8 were waited for; matrix products, arithmetic and copies ran while one was open for 37% of the time, Pallas kernels for 0%

profile of v1, /device:TPU:0, one launch (start us, length us, event | category | flops | bytes accessed | tf_op | source)
XLA Modules:
  0.0 1331.8 jit_solution(15536964556171029865)
XLA Ops:
  48.4 10.8 fusion.39
  96.8 58.3 %all-to-all-done = bf16[4,256,3,4,256]{1,4,0,2,3:T(8,128)(2,1)} async-done(((bf16[4,256,3,4,256]{1,4,0,2,3:T(8,128)(2,1)}), bf16[4,256,3,4,256]{1,4,0,2,3:T(8,128)(2,1)}, u32[]{:S(2)}, u32[]{:S(2)}) %all-to-all-start) | async-done | bytes 6291488 | tf_op jit(solution)/shard_map/all_to_all | solution.py:124
  165.4 11.0 reshape.385
  176.4 60.7 %while.22 = (s32[]{:T(128)}, bf16[4,1024,4,64]{1,3,2,0:T(8,128)(2,1)}, f32[4,4,1024]{2,1,0:T(4,128)}, bf16[4,1024,3,4,64]{1,4,3,2,0:T(8,128)(2,1)}, s32[4,1024]{1,0:T(4,128)S(1)}, /*index=5*/s32[]{:T(128)}) while((s32[]{:T(128)}, bf16[4,1024,4,64]{1,3,2,0:T(8,128)(2,1)}, f32[4,4,1024]{2,1,0:T(4,128)}, bf16[4,1024,3,4,64]{1,4,3,2,0:T(8,128)(2,1)}, ...), condition=%wide.region_5.6_spmd, body=%wide.region_2.5_spmd.sunk | while | flops 1127477248 | bytes 59913292 | solution.py:127
  246.0 208.5 %while.23 = (s32[]{:T(128)}, bf16[4,1024,3,4,64]{1,4,3,2,0:T(8,128)(2,1)}, bf16[4,1024,3,4,64]{1,4,3,2,0:T(8,128)(2,1)}, s32[4,1024]{1,0:T(4,128)S(1)}, f32[4,4,...) while((s32[]{:T(128)}, bf16[4,1024,3,4,64]{1,4,3,2,0:T(8,128)(2,1)}, ...), condition=%wide.region_8.9_spmd, body=%wide.region_6.8_spmd.sunk | while | flops 2731274240 | bytes 196179696 | solution.py:162
  258.5 12.7 multiply_reduce_fusion.5
  271.2 11.9 multiply_convert_fusion.5
  310.6 12.7 multiply_reduce_fusion.5
  323.3 11.9 multiply_convert_fusion.5
  362.7 12.7 multiply_reduce_fusion.5
  375.4 11.9 multiply_convert_fusion.5
  414.8 12.7 multiply_reduce_fusion.5
  427.5 11.9 multiply_convert_fusion.5
  454.5 10.8 copy.118
  480.9 82.8 %all-to-all-done.3 = bf16[4,1024,3,1,256]{4,0,3,2,1:T(4,128)(2,1)} async-done(((bf16[4,1024,3,1,256]{4,0,3,2,1:T(4,128)(2,1)}), bf16[4,1024,3,1,256]{4,0,3,2,1:T(4,128)(2,1)}, u32[]{:S(2)}, u32[]{:S(2)}) %all-to-all-start.3) | async-done | bytes 6291488 | tf_op jit(solution)/shard_map/all_to_all | solution.py:164
  573.6 12.6 copy.120
  609.6 11.6 copy.121
  638.1 18.6 %fusion.48 = f32[1024,4096]{1,0:T(8,128)} fusion(bf16[1024,1024]{1,0:T(8,128)(2,1)} %bitcast.215, bf16[1024,4096]{1,0:T(8,128)(2,1)} %param.21), kind=kOutput, calls=%fused_computation.117 | convolution fusion | flops 8589934592 | bytes 27262976 | tf_op jit(solution)/shard_map/dot_general | solution.py:138
  656.8 26.5 %convert_reduce_fusion = (f32[4096]{0:T(1024)S(1)}, bf16[1024,4096]{1,0:T(8,128)(2,1)}) fusion(f32[1024,4096]{1,0:T(8,128)} %fusion.48, f32[4096]{0:T(1024)S(1)} %copy-done.28, bf16[1024,1024]{1,0:T(8,128)(2,1)} %copy-done.9, bf16[4096,1024]{1,0:T(8,128)(2,1)} %param.23), kind=kOutput, calls=%fused_computation.59 | convolution fusion | flops 8686399488 | bytes 35684352 | tf_op jit(solution)/shard_map/td,fd->tf/dot_general | solution.py:152
  683.3 16.4 %fusion.52 = f32[1024,4096]{1,0:T(8,128)} fusion(bf16[1024,1024]{1,0:T(8,128)(2,1)} %bitcast.216, bf16[1024,4096]{1,0:T(8,128)(2,1)} %get-tuple-element.108), kind=kOutput, calls=%fused_computation.121 | convolution fusion | flops 8589934592 | bytes 27262976 | tf_op jit(solution)/shard_map/td,tf->df/dot_general | solution.py:155
  699.7 20.1 %fusion.43 = f32[4096,1024]{1,0:T(8,128)} fusion(bf16[1024,1024]{1,0:T(8,128)(2,1)} %copy-done.9, f32[1024,4096]{1,0:T(8,128)} %fusion.48, f32[4096]{0:T(1024)S(1)} %copy-done.28), kind=kOutput, calls=%fused_computation.113 | convolution fusion | flops 8631877632 | bytes 35667968 | tf_op jit(solution)/shard_map/tf,td->fd/dot_general | solution.py:149
  720.5 17.9 %reduce-scatter.9.cloned.1.call-done = f32[1024,768]{1,0:T(8,128)} async-done(((f32[1024,3072]{1,0:T(8,128)}), f32[1024,768]{1,0:T(8,128)}) %reduce-scatter.9.cloned.1.call-update) | async-done | bytes 3145744 | tf_op jit(solution)/shard_map/reduce_scatter | solution.py:178
  738.4 128.9 %reduce-scatter.17.cloned.1.call-done = f32[1024,1024]{1,0:T(8,128)} async-done(((f32[1024,4096]{1,0:T(8,128)}), f32[1024,1024]{1,0:T(8,128)}) %reduce-scatter.17.cloned.1.call-update) | async-done | bytes 4194320 | tf_op jit(solution)/shard_map/reduce_scatter | solution.py:180
  873.3 122.6 %reduce-scatter.21.cloned.1.call-done = f32[4096,256]{1,0:T(8,128)} async-done(((f32[4096,1024]{1,0:T(8,128)}), f32[4096,256]{1,0:T(8,128)}) %reduce-scatter.21.cloned.1.call-update) | async-done | bytes 4194320 | tf_op jit(solution)/shard_map/reduce_scatter | solution.py:181
  995.9 19.7 %fusion.38 = bf16[1024,1024]{1,0:T(8,128)(2,1)} fusion(f32[1024,1024]{1,0:T(8,128)} %fusion.47, bf16[4,256,1024]{2,1,0:T(8,128)(2,1)} %param.16, f32[1024]{0:T(1024)S(1)} %copy-done.29, bf16[4096,1024]{1,0:T(8,128)(2,1)} %param.23, f32[1024,4096]{1,0:T(8,128)} %fusion.48, f32[4096]{0:T(1024)S(1)} %copy-done.28), kind=kOutput, calls=%fused_computation.74 | convolution fusion | flops 8637120512 | bytes 33574912 | tf_op jit(solution)/shard_map/dot_general | solution.py:141
  1015.6 10.7 fusion.49
  1026.4 14.2 %fusion.46 = (f32[1024]{0:T(1024)S(1)}, f32[1024,1024]{1,0:T(8,128)S(1)}) fusion(f32[1024,1024]{1,0:T(8,128)S(1)} %fusion.49, bf16[1024,4096]{1,0:T(8,128)(2,1)} %get-tuple-element.108, bf16[1024,4096]{1,0:T(8,128)(2,1)} %param.21), kind=kOutput, calls=%fused_computation.115 | convolution fusion | flops 8592030720 | bytes 25169920 | tf_op jit(solution)/shard_map/tf,df->td/dot_general | solution.py:169
  1043.6 10.3 all-reduce.10
  1053.9 38.5 %all-reduce.9 = (f32[1024]{0:T(1024)}, f32[1024]{0:T(1024)}, f32[4096]{0:T(1024)}, f32[1024]{0:T(1024)}) all-reduce(f32[1024]{0:T(1024)S(1)} %get-tuple-element.101, f32[1024]{0:T(1024)S(1)} %get-tuple-element.102, f32[4096]{0:T(1024)S(1)} %get-tuple-element.103, ...), channel_id=1, replica_groups=mesh['dp'=8,'seq'=4] {'dp'}, use_global_device_ids=true, to_apply=%region_13.14 | all-reduce | flops 7168 | bytes 57344 | tf_op jit(solution)/shard_map/psum | solution.py:174
  1098.0 43.0 %reduce-scatter.11.cloned.1.call-done = f32[128,768]{1,0:T(8,128)} async-done(((f32[1024,768]{1,0:T(8,128)}), f32[128,768]{1,0:T(8,128)}) %reduce-scatter.11.cloned.1.call-update) | async-done | bytes 393232 | tf_op jit(solution)/shard_map/reduce_scatter | solution.py:184
  1141.0 91.4 %reduce-scatter.19.cloned.1.call-done = f32[128,1024]{1,0:T(8,128)} async-done(((f32[1024,1024]{1,0:T(8,128)}), f32[128,1024]{1,0:T(8,128)}) %reduce-scatter.19.cloned.1.call-update) | async-done | bytes 524304 | tf_op jit(solution)/shard_map/reduce_scatter | solution.py:186
  1232.4 92.3 %reduce-scatter.23.cloned.1.call-done = f32[512,256]{1,0:T(8,128)} async-done(((f32[4096,256]{1,0:T(8,128)}), f32[512,256]{1,0:T(8,128)}) %reduce-scatter.23.cloned.1.call-update) | async-done | bytes 524304 | tf_op jit(solution)/shard_map/reduce_scatter | solution.py:187
  (245 shorter events, 349.3 us)
Async XLA Ops:
  26.4 51.6 %all-to-all-start.2 = ((bf16[4,256,4,256]{3,1,0,2:T(8,128)(2,1)}), bf16[4,256,4,256]{3,1,0,2:T(8,128)(2,1)}, u32[]{:S(2)}, u32[]{:S(2)}) async-start(bf16[4,256,4,256]{3,1,0,2:T(8,128)(2,1)} %copy.116), calls=%async_computation.2 | async-start | bytes 4194304 | tf_op jit(solution)/shard_map/all_to_all | solution.py:160
  33.1 11.6 copy-start.17
  78.0 77.2 %all-to-all-start = ((bf16[4,256,3,4,256]{1,4,0,2,3:T(8,128)(2,1)}), bf16[4,256,3,4,256]{1,4,0,2,3:T(8,128)(2,1)}, u32[]{:S(2)}, u32[]{:S(2)}) async-start(bf16[4,256,3,4,256]{1,4,0,2,3:T(8,128)(2,1)} %copy.127), calls=%async_computation | async-start | bytes 12582912 | tf_op jit(solution)/shard_map/all_to_all | solution.py:124
  165.4 11.0 copy-start.19
  241.4 223.9 %all-to-all-start.1 = ((bf16[4,1024,1,256]{3,0,2,1:T(4,128)(2,1)}), bf16[4,1024,1,256]{3,0,2,1:T(4,128)(2,1)}, u32[]{:S(2)}, u32[]{:S(2)}) async-start(bf16[4,1024,1,256]{3,0,2,1:T(4,128)(2,1)} %copy.113), calls=%async_computation.1 | async-start | bytes 4194304 | tf_op jit(solution)/shard_map/all_to_all | solution.py:129
  271.2 20.0 %slice-start = ((s8[16777216]{0:T(1024)(128)(4,1)}), s8[4194304]{0:T(1024)(128)(4,1)S(1)}, s32[]{:S(2)}) async-start(s8[16777216]{0:T(1024)(128)(4,1)} %bitcast.198), calls=%async_computation.20 | async-start | bytes 8388608 | tf_op jit(solution)/shard_map/while
  271.2 20.0 %slice-start.1 = ((s8[16777216]{0:T(1024)(128)(4,1)}), s8[4194304]{0:T(1024)(128)(4,1)S(1)}, s32[]{:S(2)}) async-start(s8[16777216]{0:T(1024)(128)(4,1)} %bitcast.198), calls=%async_computation.21 | async-start | bytes 8388608 | tf_op jit(solution)/shard_map/while
  271.2 20.0 %slice-start.2 = ((s8[16777216]{0:T(1024)(128)(4,1)}), s8[4194304]{0:T(1024)(128)(4,1)S(1)}, s32[]{:S(2)}) async-start(s8[16777216]{0:T(1024)(128)(4,1)} %bitcast.198), calls=%async_computation.22 | async-start | bytes 8388608 | tf_op jit(solution)/shard_map/while
  299.7 10.9 copy-start.1
  323.3 20.0 %slice-start = ((s8[16777216]{0:T(1024)(128)(4,1)}), s8[4194304]{0:T(1024)(128)(4,1)S(1)}, s32[]{:S(2)}) async-start(s8[16777216]{0:T(1024)(128)(4,1)} %bitcast.198), calls=%async_computation.20 | async-start | bytes 8388608 | tf_op jit(solution)/shard_map/while
  323.3 20.0 %slice-start.1 = ((s8[16777216]{0:T(1024)(128)(4,1)}), s8[4194304]{0:T(1024)(128)(4,1)S(1)}, s32[]{:S(2)}) async-start(s8[16777216]{0:T(1024)(128)(4,1)} %bitcast.198), calls=%async_computation.21 | async-start | bytes 8388608 | tf_op jit(solution)/shard_map/while
  323.3 20.0 %slice-start.2 = ((s8[16777216]{0:T(1024)(128)(4,1)}), s8[4194304]{0:T(1024)(128)(4,1)S(1)}, s32[]{:S(2)}) async-start(s8[16777216]{0:T(1024)(128)(4,1)} %bitcast.198), calls=%async_computation.22 | async-start | bytes 8388608 | tf_op jit(solution)/shard_map/while
  375.4 20.0 %slice-start = ((s8[16777216]{0:T(1024)(128)(4,1)}), s8[4194304]{0:T(1024)(128)(4,1)S(1)}, s32[]{:S(2)}) async-start(s8[16777216]{0:T(1024)(128)(4,1)} %bitcast.198), calls=%async_computation.20 | async-start | bytes 8388608 | tf_op jit(solution)/shard_map/while
  375.4 20.0 %slice-start.1 = ((s8[16777216]{0:T(1024)(128)(4,1)}), s8[4194304]{0:T(1024)(128)(4,1)S(1)}, s32[]{:S(2)}) async-start(s8[16777216]{0:T(1024)(128)(4,1)} %bitcast.198), calls=%async_computation.21 | async-start | bytes 8388608 | tf_op jit(solution)/shard_map/while
  375.4 20.0 %slice-start.2 = ((s8[16777216]{0:T(1024)(128)(4,1)}), s8[4194304]{0:T(1024)(128)(4,1)S(1)}, s32[]{:S(2)}) async-start(s8[16777216]{0:T(1024)(128)(4,1)} %bitcast.198), calls=%async_computation.22 | async-start | bytes 8388608 | tf_op jit(solution)/shard_map/while
  427.5 20.0 %slice-start = ((s8[16777216]{0:T(1024)(128)(4,1)}), s8[4194304]{0:T(1024)(128)(4,1)S(1)}, s32[]{:S(2)}) async-start(s8[16777216]{0:T(1024)(128)(4,1)} %bitcast.198), calls=%async_computation.20 | async-start | bytes 8388608 | tf_op jit(solution)/shard_map/while
  427.5 20.0 %slice-start.1 = ((s8[16777216]{0:T(1024)(128)(4,1)}), s8[4194304]{0:T(1024)(128)(4,1)S(1)}, s32[]{:S(2)}) async-start(s8[16777216]{0:T(1024)(128)(4,1)} %bitcast.198), calls=%async_computation.21 | async-start | bytes 8388608 | tf_op jit(solution)/shard_map/while
  427.5 20.0 %slice-start.2 = ((s8[16777216]{0:T(1024)(128)(4,1)}), s8[4194304]{0:T(1024)(128)(4,1)S(1)}, s32[]{:S(2)}) async-start(s8[16777216]{0:T(1024)(128)(4,1)} %bitcast.198), calls=%async_computation.22 | async-start | bytes 8388608 | tf_op jit(solution)/shard_map/while
  465.3 98.4 %all-to-all-start.3 = ((bf16[4,1024,3,1,256]{4,0,3,2,1:T(4,128)(2,1)}), bf16[4,1024,3,1,256]{4,0,3,2,1:T(4,128)(2,1)}, u32[]{:S(2)}, u32[]{:S(2)}) async-start(bf16[4,1024,3,1,256]{4,0,3,2,1:T(4,128)(2,1)} %copy.118), calls=%async_computation.3 | async-start | bytes 12582912 | tf_op jit(solution)/shard_map/all_to_all | solution.py:164
  470.5 249.4 %reduce-scatter.13.cloned.1.call-start = ((), (), s32[]{:S(2)}) async-start(), calls=%async_computation.14 | async-start | bytes 5242880 | tf_op jit(solution)/shard_map/reduce_scatter | solution.py:179
  480.8 257.5 %reduce-scatter.9.cloned.1.call-start = ((), (), s32[]{:S(2)}) async-start(), calls=%async_computation.12 | async-start | bytes 15728640 | tf_op jit(solution)/shard_map/reduce_scatter | solution.py:178
  638.1 18.7 %copy-start.28 = (f32[4096]{0:T(1024)S(1)}, f32[4096]{0:T(1024)}, u32[]{:S(2)}) copy-start(f32[4096]{0:T(1024)} %param.22) | copy-start | bytes 49156
  638.1 229.2 %reduce-scatter.17.cloned.1.call-start = ((), (), s32[]{:S(2)}) async-start(), calls=%async_computation.16 | async-start | bytes 20971520 | tf_op jit(solution)/shard_map/reduce_scatter | solution.py:180
  699.6 296.2 %reduce-scatter.21.cloned.1.call-start = ((), (), s32[]{:S(2)}) async-start(), calls=%async_computation.18 | async-start | bytes 20971520 | tf_op jit(solution)/shard_map/reduce_scatter | solution.py:181
  719.8 378.2 %reduce-scatter.15.cloned.1.call-start = ((), (), s32[]{:S(2)}) async-start(), calls=%async_computation.15 | async-start | bytes 1179648 | tf_op jit(solution)/shard_map/reduce_scatter | solution.py:185
  720.4 420.6 %reduce-scatter.11.cloned.1.call-start = ((), (), s32[]{:S(2)}) async-start(), calls=%async_computation.13 | async-start | bytes 3538944 | tf_op jit(solution)/shard_map/reduce_scatter | solution.py:184
  738.4 494.0 %reduce-scatter.19.cloned.1.call-start = ((), (), s32[]{:S(2)}) async-start(), calls=%async_computation.17 | async-start | bytes 4718592 | tf_op jit(solution)/shard_map/reduce_scatter | solution.py:186
  867.3 457.4 %reduce-scatter.23.cloned.1.call-start = ((), (), s32[]{:S(2)}) async-start(), calls=%async_computation.19 | async-start | bytes 4718592 | tf_op jit(solution)/shard_map/reduce_scatter | solution.py:187
  873.3 122.6 %copy-start.29 = (f32[1024]{0:T(1024)S(1)}, f32[1024]{0:T(1024)}, u32[]{:S(2)}) copy-start(f32[1024]{0:T(1024)} %param.24) | copy-start | bytes 12292
  1026.3 14.2 %copy-start.2 = (bf16[4,256,1024]{2,1,0:T(8,128)(2,1)S(1)}, bf16[4,256,1024]{2,1,0:T(8,128)(2,1)}, u32[]{:S(2)}) copy-start(bf16[4,256,1024]{2,1,0:T(8,128)(2,1)} %param.16) | copy-start | bytes 6291460
  1026.4 14.2 %copy-start.18 = (f32[4,256]{1,0:T(4,128)S(1)}, f32[4,256]{1,0:T(4,128)}, u32[]{:S(2)}) copy-start(f32[4,256]{1,0:T(4,128)} %copy-done.17) | copy-start | bytes 12292
  1026.4 14.2 %copy-start.23 = (f32[1024]{0:T(1024)S(1)}, f32[1024]{0:T(1024)}, u32[]{:S(2)}) copy-start(f32[1024]{0:T(1024)} %param.17) | copy-start | bytes 12292
  (29 other events, 143.2 us)
Sparse Core Ops, SparseCore 0:
  480.9 69.5 reduce-scatter.12
  638.2 100.0 reduce-scatter.8
  741.1 126.1 reduce-scatter.16
  869.7 126.1 reduce-scatter.20
  1000.1 63.3 reduce-scatter.14
  1067.5 73.4 reduce-scatter.10
  1145.2 87.1 reduce-scatter.18
  1237.0 87.6 reduce-scatter.22
